TPU v7x, 32 devices: a whole 2x2x4 slice. The times are simulated.
32 devices in a mesh: aa: 8 (over z, x), ba: 4 (over y, core).
Axes of the slice: x: 2, y: 2, z: 4, core: 2. Of those that a mesh axis runs over, the one named last changes fastest.
Arguments:
- patches: bfloat16 [8, 64, 512], P('ba'), may hold values from -6 to 6
- token_first: bfloat16 [8, 64, 256], P('aa'), may hold values from -0.75 to 0.75
- token_second: bfloat16 [8, 64, 256], P('aa'), may hold values from -0.375 to 0.375
- channel_first: bfloat16 [8, 512, 2048], P('aa'), may hold values from -0.25 to 0.25
- channel_second: bfloat16 [8, 2048, 512], P('aa'), may hold values from -0.1875 to 0.1875
- gains: float32 [8, 2, 512], P('aa'), may hold values from 0.25 to 1.75
- final_gain: float32 [512], replicated, may hold values from 0.25 to 1.75
- head_weight: bfloat16 [512, 1000], replicated, may hold values from -2 to 2
- depths: int32 [16, 2], replicated, may hold values from 1 to 4
- widths: int32 [16, 8], replicated, may hold values from 1 to 4
- labels: int32 [8], P('ba'), may hold values from 0 to 999
Outputs:
- losses: float32 [16], replicated
All inputs are finite; a program needn't handle non-finite values.
Results may differ from a plain program's by a relative error of at most 0.0012.
Values may be sent and summed in bfloat16 or wider, within the bound.
A program may use at most 64 MiB of HBM per device.

v0:
```python
import jax
import jax.numpy as jnp
from jax import lax
from jax.sharding import PartitionSpec as P

UNIT = 4


def from_behind(value, axis, steps):
    count = lax.axis_size(axis)
    first, last = (max(0, -steps), min(count, count - steps))
    return lax.ppermute(value, axis, [(source, source + steps) for source in range(first, last)])


def layer_norm(values, gain):
    center = values - jnp.mean(values, axis=-1, keepdims=True)
    spread = jnp.mean(center * center, axis=-1, keepdims=True)
    return center * lax.rsqrt(spread + 1e-06) * gain


def mixer_block(
    state, token_first_weight, token_second_weight, channel_one, channel_two, gain_pair, width
):
    floats = state.astype(jnp.float32)
    normalized_input = layer_norm(floats, gain_pair[0]).astype(jnp.bfloat16)
    token_before_mixing = jnp.einsum(
        "gtc,tp->gpc", normalized_input, token_first_weight, preferred_element_type=jnp.float32
    )
    token_mixing_hidden = jax.nn.gelu(token_before_mixing, approximate=True).astype(jnp.bfloat16)
    token_portion = jnp.einsum(
        "hcx,mc->hmx", token_mixing_hidden, token_second_weight, preferred_element_type=jnp.float32
    )
    mixed = floats + token_portion
    second = layer_norm(mixed, gain_pair[1]).astype(jnp.bfloat16)
    rows = second.reshape(-1, mixed.shape[2])
    channel_pre = jnp.dot(rows, channel_one, preferred_element_type=jnp.float32)
    hidden_units = channel_one.shape[1]
    lanes = jnp.arange(hidden_units)
    keep = lanes < width * (hidden_units // 4)
    channel_hidden = jnp.where(
        keep[None, :], jax.nn.gelu(channel_pre, approximate=True), 0.0
    ).astype(jnp.bfloat16)
    channel_portion = jnp.dot(channel_hidden, channel_two, preferred_element_type=jnp.float32)
    return (mixed + channel_portion.reshape(mixed.shape)).astype(jnp.bfloat16)


def head_loss(state, final_gain, head_weight, labels):
    normalized_input = layer_norm(state.astype(jnp.float32), final_gain)
    pooled = jnp.mean(normalized_input, axis=1).astype(jnp.bfloat16)
    logits = jnp.dot(pooled, head_weight, preferred_element_type=jnp.float32)
    total = jax.nn.logsumexp(logits, axis=-1)
    classes = jnp.arange(head_weight.shape[1])
    picked = jnp.sum(jnp.where(classes[None, :] == labels[:, None], logits, 0.0), axis=-1)
    return jnp.sum(total - picked)


def local(
    patches,
    token_first,
    token_second,
    channel_first,
    channel_second,
    gains,
    final_gain,
    head_weight,
    depths,
    widths,
    labels,
):
    section = lax.axis_index("aa")
    section_count = lax.axis_size("aa")
    candidates = depths.shape[0]
    unit_pick = jnp.arange(depths.shape[1]) == section // UNIT
    depth_here = jnp.sum(jnp.where(unit_pick[None, :], depths, 0), axis=1)
    section_pick = jnp.arange(widths.shape[1]) == section
    width_here = jnp.sum(jnp.where(section_pick[None, :], widths, 0), axis=1)
    active_here = section % UNIT < depth_here
    groups = 1
    block_rows = patches.shape[0] // groups
    micro_count = candidates * groups
    steps_total = micro_count + section_count - 1
    token_first_weight = token_first[0]
    token_second_weight = token_second[0]
    channel_one = channel_first[0]
    channel_two = channel_second[0]
    gain_pair = gains[0]
    slot_ids = jnp.arange(candidates)

    def advance(step, carry):
        outgoing, totals = carry
        received = from_behind(outgoing, "aa", 1)
        micro = step - section
        valid = jnp.logical_and(micro >= 0, micro < micro_count)
        clipped = jnp.clip(micro, 0, micro_count - 1)
        candidate = clipped // groups
        inputs = jnp.where(section == 0, patches, received)
        active = active_here[candidate]
        width = width_here[candidate]
        computed = mixer_block(
            inputs,
            token_first_weight,
            token_second_weight,
            channel_one,
            channel_two,
            gain_pair,
            width,
        )
        updated = jnp.where(active, computed, inputs)
        loss_part = head_loss(updated, final_gain, head_weight, labels)
        counted = jnp.logical_and(valid, section == section_count - 1)
        loss_part = jnp.where(counted, loss_part, 0.0)
        totals = totals + jnp.where(slot_ids == candidate, loss_part, 0.0)
        return (updated, totals)

    start = (
        jnp.zeros((block_rows,) + patches.shape[1:], jnp.bfloat16),
        jnp.zeros((candidates,), jnp.float32),
    )
    final_state, totals = lax.fori_loop(0, steps_total, advance, start)
    return lax.psum(totals, ("aa", "ba"))


def solution(mesh):
    return jax.shard_map(
        local,
        mesh=mesh,
        in_specs=(
            P("ba", None, None),
            P("aa", None, None),
            P("aa", None, None),
            P("aa", None, None),
            P("aa", None, None),
            P("aa", None, None),
            P(),
            P(),
            P(),
            P(),
            P("ba"),
        ),
        out_specs=P(),
        check_vma=False,
    )
```

profile of v0, /device:TPU:0, one launch (start us, length us, event | category | flops | bytes accessed | tf_op | source)
XLA Modules:
  0.0 427.6 jit_solution(14116178011746971400)
XLA Ops:
  1.6 384.1 %while.18 = (s32[]{:T(128)}, bf16[2,64,512]{2,1,0:T(8,128)(2,1)S(1)}, f32[16]{0:T(128)S(1)}, s32[]{:T(128)}, pred[16]{0:T(512)(128)(4,1)S(1)}, /*index=5*/pred[]...) while((s32[]{:T(128)}, ...), condition=%wide.region_14.15_spmd.clone, body=%wide.region_2.14_spmd.clone.sunk | while | flops 613448832 | bytes 13246269 | solution.py:119
  1.6 4.9 %collective-permute-start = (bf16[2,64,512]{2,1,0:T(8,128)(2,1)S(1)}, bf16[2,64,512]{2,1,0:T(8,128)(2,1)S(1)}, u32[]{:S(2)}, u32[]{:S(2)}) collective-permute-start(bf16[2,64,512]{2,1,0:T(8,128)(2,1)S(1)} %broadcast_select_fusion.5), channel_id=1, source_target_pairs={{0,4},{4,8},{8,12},{12,16},{16,20},{20,24},{24,28},{1,5},{5,9},{9,... | collective-permute-start | bytes 393224 | tf_op jit(solution)/shard_map/while/body/eval_jaxpr/ppermute | solution.py:12
  12.5 3.3 fusion.107
  19.0 3.5 collective-permute-start
  28.5 3.3 fusion.107
  35.0 3.5 collective-permute-start
  44.4 3.3 fusion.107
  50.9 4.2 collective-permute-start
  61.0 3.3 fusion.107
  67.5 4.2 collective-permute-start
  77.7 3.3 fusion.107
  84.2 4.2 collective-permute-start
  94.3 3.3 fusion.107
  100.8 4.2 collective-permute-start
  111.0 3.3 fusion.107
  117.5 4.2 collective-permute-start
  127.6 3.3 fusion.107
  134.1 4.2 collective-permute-start
  144.3 3.3 fusion.107
  150.8 4.2 collective-permute-start
  160.9 3.3 fusion.107
  167.4 4.2 collective-permute-start
  177.5 3.3 fusion.107
  184.1 4.2 collective-permute-start
  194.2 3.3 fusion.107
  200.7 4.2 collective-permute-start
  210.8 3.3 fusion.107
  217.3 4.5 %collective-permute-start = (bf16[2,64,512]{2,1,0:T(8,128)(2,1)S(1)}, bf16[2,64,512]{2,1,0:T(8,128)(2,1)S(1)}, u32[]{:S(2)}, u32[]{:S(2)}) collective-permute-start(bf16[2,64,512]{2,1,0:T(8,128)(2,1)S(1)} %broadcast_select_fusion.5), channel_id=1, source_target_pairs={{0,4},{4,8},{8,12},{12,16},{16,20},{20,24},{24,28},{1,5},{5,9},{9,... | collective-permute-start | bytes 393224 | tf_op jit(solution)/shard_map/while/body/eval_jaxpr/ppermute | solution.py:12
  228.7 3.3 fusion.107
  235.2 4.4 %collective-permute-start = (bf16[2,64,512]{2,1,0:T(8,128)(2,1)S(1)}, bf16[2,64,512]{2,1,0:T(8,128)(2,1)S(1)}, u32[]{:S(2)}, u32[]{:S(2)}) collective-permute-start(bf16[2,64,512]{2,1,0:T(8,128)(2,1)S(1)} %broadcast_select_fusion.5), channel_id=1, source_target_pairs={{0,4},{4,8},{8,12},{12,16},{16,20},{20,24},{24,28},{1,5},{5,9},{9,... | collective-permute-start | bytes 393224 | tf_op jit(solution)/shard_map/while/body/eval_jaxpr/ppermute | solution.py:12
  245.6 3.3 fusion.107
  252.1 4.4 %collective-permute-start = (bf16[2,64,512]{2,1,0:T(8,128)(2,1)S(1)}, bf16[2,64,512]{2,1,0:T(8,128)(2,1)S(1)}, u32[]{:S(2)}, u32[]{:S(2)}) collective-permute-start(bf16[2,64,512]{2,1,0:T(8,128)(2,1)S(1)} %broadcast_select_fusion.5), channel_id=1, source_target_pairs={{0,4},{4,8},{8,12},{12,16},{16,20},{20,24},{24,28},{1,5},{5,9},{9,... | collective-permute-start | bytes 393224 | tf_op jit(solution)/shard_map/while/body/eval_jaxpr/ppermute | solution.py:12
  262.5 3.3 fusion.107
  269.0 4.4 %collective-permute-start = (bf16[2,64,512]{2,1,0:T(8,128)(2,1)S(1)}, bf16[2,64,512]{2,1,0:T(8,128)(2,1)S(1)}, u32[]{:S(2)}, u32[]{:S(2)}) collective-permute-start(bf16[2,64,512]{2,1,0:T(8,128)(2,1)S(1)} %broadcast_select_fusion.5), channel_id=1, source_target_pairs={{0,4},{4,8},{8,12},{12,16},{16,20},{20,24},{24,28},{1,5},{5,9},{9,... | collective-permute-start | bytes 393224 | tf_op jit(solution)/shard_map/while/body/eval_jaxpr/ppermute | solution.py:12
  279.3 3.3 fusion.107
  285.9 4.2 collective-permute-start
  296.0 3.3 fusion.107
  302.5 4.2 collective-permute-start
  312.6 3.3 fusion.107
  319.1 4.2 collective-permute-start
  329.3 3.3 fusion.107
  335.8 4.2 collective-permute-start
  345.9 3.3 fusion.107
  352.4 4.2 collective-permute-start
  362.6 3.3 fusion.107
  369.1 4.2 collective-permute-start
  379.2 3.3 fusion.107
  385.7 41.9 %psum.7 = f32[16]{0:T(128)} all-reduce(f32[16]{0:T(128)S(1)} %get-tuple-element.392), channel_id=1, replica_groups=mesh['aa'=8,'ba'=4] {'aa','ba'}, use_global_device_ids=true, to_apply=%region_15.16 | all-reduce | flops 16 | bytes 128 | tf_op jit(solution)/shard_map/psum | solution.py:120
  (720 shorter events, 181.9 us)
Async XLA Ops:
  1.6 7.6 %collective-permute-start = (bf16[2,64,512]{2,1,0:T(8,128)(2,1)S(1)}, bf16[2,64,512]{2,1,0:T(8,128)(2,1)S(1)}, u32[]{:S(2)}, u32[]{:S(2)}) collective-permute-start(bf16[2,64,512]{2,1,0:T(8,128)(2,1)S(1)} %broadcast_select_fusion.5), channel_id=1, source_target_pairs={{0,4},{4,8},{8,12},{12,16},{16,20},{20,24},{24,28},{1,5},{5,9},{9,... | collective-permute-start | bytes 393224 | tf_op jit(solution)/shard_map/while/body/eval_jaxpr/ppermute | solution.py:12
  12.5 4.3 %copy-start.1 = (f32[512]{0:T(512)S(1)}, f32[512]{0:T(512)}, u32[]{:S(2)}) copy-start(f32[512]{0:T(512)} %get-tuple-element.682) | copy-start | bytes 6148 | tf_op jit(solution)/shard_map/while
  12.5 4.4 %copy-start = (bf16[512,1000]{0,1:T(8,128)(2,1)S(1)}, bf16[512,1000]{0,1:T(8,128)(2,1)}, u32[]{:S(2)}) copy-start(bf16[512,1000]{0,1:T(8,128)(2,1)} %get-tuple-element.683) | copy-start | bytes 3072004 | tf_op jit(solution)/shard_map/while
  19.0 6.2 %collective-permute-start = (bf16[2,64,512]{2,1,0:T(8,128)(2,1)S(1)}, bf16[2,64,512]{2,1,0:T(8,128)(2,1)S(1)}, u32[]{:S(2)}, u32[]{:S(2)}) collective-permute-start(bf16[2,64,512]{2,1,0:T(8,128)(2,1)S(1)} %broadcast_select_fusion.5), channel_id=1, source_target_pairs={{0,4},{4,8},{8,12},{12,16},{16,20},{20,24},{24,28},{1,5},{5,9},{9,... | collective-permute-start | bytes 393224 | tf_op jit(solution)/shard_map/while/body/eval_jaxpr/ppermute | solution.py:12
  28.4 4.3 %copy-start.1 = (f32[512]{0:T(512)S(1)}, f32[512]{0:T(512)}, u32[]{:S(2)}) copy-start(f32[512]{0:T(512)} %get-tuple-element.682) | copy-start | bytes 6148 | tf_op jit(solution)/shard_map/while
  28.4 4.4 %copy-start = (bf16[512,1000]{0,1:T(8,128)(2,1)S(1)}, bf16[512,1000]{0,1:T(8,128)(2,1)}, u32[]{:S(2)}) copy-start(bf16[512,1000]{0,1:T(8,128)(2,1)} %get-tuple-element.683) | copy-start | bytes 3072004 | tf_op jit(solution)/shard_map/while
  35.0 6.1 %collective-permute-start = (bf16[2,64,512]{2,1,0:T(8,128)(2,1)S(1)}, bf16[2,64,512]{2,1,0:T(8,128)(2,1)S(1)}, u32[]{:S(2)}, u32[]{:S(2)}) collective-permute-start(bf16[2,64,512]{2,1,0:T(8,128)(2,1)S(1)} %broadcast_select_fusion.5), channel_id=1, source_target_pairs={{0,4},{4,8},{8,12},{12,16},{16,20},{20,24},{24,28},{1,5},{5,9},{9,... | collective-permute-start | bytes 393224 | tf_op jit(solution)/shard_map/while/body/eval_jaxpr/ppermute | solution.py:12
  44.4 4.4 %copy-start = (bf16[512,1000]{0,1:T(8,128)(2,1)S(1)}, bf16[512,1000]{0,1:T(8,128)(2,1)}, u32[]{:S(2)}) copy-start(bf16[512,1000]{0,1:T(8,128)(2,1)} %get-tuple-element.683) | copy-start | bytes 3072004 | tf_op jit(solution)/shard_map/while
  50.9 6.8 %collective-permute-start = (bf16[2,64,512]{2,1,0:T(8,128)(2,1)S(1)}, bf16[2,64,512]{2,1,0:T(8,128)(2,1)S(1)}, u32[]{:S(2)}, u32[]{:S(2)}) collective-permute-start(bf16[2,64,512]{2,1,0:T(8,128)(2,1)S(1)} %broadcast_select_fusion.5), channel_id=1, source_target_pairs={{0,4},{4,8},{8,12},{12,16},{16,20},{20,24},{24,28},{1,5},{5,9},{9,... | collective-permute-start | bytes 393224 | tf_op jit(solution)/shard_map/while/body/eval_jaxpr/ppermute | solution.py:12
  61.0 4.4 %copy-start = (bf16[512,1000]{0,1:T(8,128)(2,1)S(1)}, bf16[512,1000]{0,1:T(8,128)(2,1)}, u32[]{:S(2)}) copy-start(bf16[512,1000]{0,1:T(8,128)(2,1)} %get-tuple-element.683) | copy-start | bytes 3072004 | tf_op jit(solution)/shard_map/while
  67.5 6.8 %collective-permute-start = (bf16[2,64,512]{2,1,0:T(8,128)(2,1)S(1)}, bf16[2,64,512]{2,1,0:T(8,128)(2,1)S(1)}, u32[]{:S(2)}, u32[]{:S(2)}) collective-permute-start(bf16[2,64,512]{2,1,0:T(8,128)(2,1)S(1)} %broadcast_select_fusion.5), channel_id=1, source_target_pairs={{0,4},{4,8},{8,12},{12,16},{16,20},{20,24},{24,28},{1,5},{5,9},{9,... | collective-permute-start | bytes 393224 | tf_op jit(solution)/shard_map/while/body/eval_jaxpr/ppermute | solution.py:12
  77.7 4.4 %copy-start = (bf16[512,1000]{0,1:T(8,128)(2,1)S(1)}, bf16[512,1000]{0,1:T(8,128)(2,1)}, u32[]{:S(2)}) copy-start(bf16[512,1000]{0,1:T(8,128)(2,1)} %get-tuple-element.683) | copy-start | bytes 3072004 | tf_op jit(solution)/shard_map/while
  84.2 6.8 %collective-permute-start = (bf16[2,64,512]{2,1,0:T(8,128)(2,1)S(1)}, bf16[2,64,512]{2,1,0:T(8,128)(2,1)S(1)}, u32[]{:S(2)}, u32[]{:S(2)}) collective-permute-start(bf16[2,64,512]{2,1,0:T(8,128)(2,1)S(1)} %broadcast_select_fusion.5), channel_id=1, source_target_pairs={{0,4},{4,8},{8,12},{12,16},{16,20},{20,24},{24,28},{1,5},{5,9},{9,... | collective-permute-start | bytes 393224 | tf_op jit(solution)/shard_map/while/body/eval_jaxpr/ppermute | solution.py:12
  94.3 4.4 %copy-start = (bf16[512,1000]{0,1:T(8,128)(2,1)S(1)}, bf16[512,1000]{0,1:T(8,128)(2,1)}, u32[]{:S(2)}) copy-start(bf16[512,1000]{0,1:T(8,128)(2,1)} %get-tuple-element.683) | copy-start | bytes 3072004 | tf_op jit(solution)/shard_map/while
  100.8 6.8 %collective-permute-start = (bf16[2,64,512]{2,1,0:T(8,128)(2,1)S(1)}, bf16[2,64,512]{2,1,0:T(8,128)(2,1)S(1)}, u32[]{:S(2)}, u32[]{:S(2)}) collective-permute-start(bf16[2,64,512]{2,1,0:T(8,128)(2,1)S(1)} %broadcast_select_fusion.5), channel_id=1, source_target_pairs={{0,4},{4,8},{8,12},{12,16},{16,20},{20,24},{24,28},{1,5},{5,9},{9,... | collective-permute-start | bytes 393224 | tf_op jit(solution)/shard_map/while/body/eval_jaxpr/ppermute | solution.py:12
  111.0 4.4 %copy-start = (bf16[512,1000]{0,1:T(8,128)(2,1)S(1)}, bf16[512,1000]{0,1:T(8,128)(2,1)}, u32[]{:S(2)}) copy-start(bf16[512,1000]{0,1:T(8,128)(2,1)} %get-tuple-element.683) | copy-start | bytes 3072004 | tf_op jit(solution)/shard_map/while
  117.5 6.8 %collective-permute-start = (bf16[2,64,512]{2,1,0:T(8,128)(2,1)S(1)}, bf16[2,64,512]{2,1,0:T(8,128)(2,1)S(1)}, u32[]{:S(2)}, u32[]{:S(2)}) collective-permute-start(bf16[2,64,512]{2,1,0:T(8,128)(2,1)S(1)} %broadcast_select_fusion.5), channel_id=1, source_target_pairs={{0,4},{4,8},{8,12},{12,16},{16,20},{20,24},{24,28},{1,5},{5,9},{9,... | collective-permute-start | bytes 393224 | tf_op jit(solution)/shard_map/while/body/eval_jaxpr/ppermute | solution.py:12
  127.6 4.4 %copy-start = (bf16[512,1000]{0,1:T(8,128)(2,1)S(1)}, bf16[512,1000]{0,1:T(8,128)(2,1)}, u32[]{:S(2)}) copy-start(bf16[512,1000]{0,1:T(8,128)(2,1)} %get-tuple-element.683) | copy-start | bytes 3072004 | tf_op jit(solution)/shard_map/while
  134.1 6.8 %collective-permute-start = (bf16[2,64,512]{2,1,0:T(8,128)(2,1)S(1)}, bf16[2,64,512]{2,1,0:T(8,128)(2,1)S(1)}, u32[]{:S(2)}, u32[]{:S(2)}) collective-permute-start(bf16[2,64,512]{2,1,0:T(8,128)(2,1)S(1)} %broadcast_select_fusion.5), channel_id=1, source_target_pairs={{0,4},{4,8},{8,12},{12,16},{16,20},{20,24},{24,28},{1,5},{5,9},{9,... | collective-permute-start | bytes 393224 | tf_op jit(solution)/shard_map/while/body/eval_jaxpr/ppermute | solution.py:12
  144.2 4.4 %copy-start = (bf16[512,1000]{0,1:T(8,128)(2,1)S(1)}, bf16[512,1000]{0,1:T(8,128)(2,1)}, u32[]{:S(2)}) copy-start(bf16[512,1000]{0,1:T(8,128)(2,1)} %get-tuple-element.683) | copy-start | bytes 3072004 | tf_op jit(solution)/shard_map/while
  150.8 6.8 %collective-permute-start = (bf16[2,64,512]{2,1,0:T(8,128)(2,1)S(1)}, bf16[2,64,512]{2,1,0:T(8,128)(2,1)S(1)}, u32[]{:S(2)}, u32[]{:S(2)}) collective-permute-start(bf16[2,64,512]{2,1,0:T(8,128)(2,1)S(1)} %broadcast_select_fusion.5), channel_id=1, source_target_pairs={{0,4},{4,8},{8,12},{12,16},{16,20},{20,24},{24,28},{1,5},{5,9},{9,... | collective-permute-start | bytes 393224 | tf_op jit(solution)/shard_map/while/body/eval_jaxpr/ppermute | solution.py:12
  160.9 4.4 %copy-start = (bf16[512,1000]{0,1:T(8,128)(2,1)S(1)}, bf16[512,1000]{0,1:T(8,128)(2,1)}, u32[]{:S(2)}) copy-start(bf16[512,1000]{0,1:T(8,128)(2,1)} %get-tuple-element.683) | copy-start | bytes 3072004 | tf_op jit(solution)/shard_map/while
  167.4 6.8 %collective-permute-start = (bf16[2,64,512]{2,1,0:T(8,128)(2,1)S(1)}, bf16[2,64,512]{2,1,0:T(8,128)(2,1)S(1)}, u32[]{:S(2)}, u32[]{:S(2)}) collective-permute-start(bf16[2,64,512]{2,1,0:T(8,128)(2,1)S(1)} %broadcast_select_fusion.5), channel_id=1, source_target_pairs={{0,4},{4,8},{8,12},{12,16},{16,20},{20,24},{24,28},{1,5},{5,9},{9,... | collective-permute-start | bytes 393224 | tf_op jit(solution)/shard_map/while/body/eval_jaxpr/ppermute | solution.py:12
  177.5 4.4 %copy-start = (bf16[512,1000]{0,1:T(8,128)(2,1)S(1)}, bf16[512,1000]{0,1:T(8,128)(2,1)}, u32[]{:S(2)}) copy-start(bf16[512,1000]{0,1:T(8,128)(2,1)} %get-tuple-element.683) | copy-start | bytes 3072004 | tf_op jit(solution)/shard_map/while
  184.1 6.8 %collective-permute-start = (bf16[2,64,512]{2,1,0:T(8,128)(2,1)S(1)}, bf16[2,64,512]{2,1,0:T(8,128)(2,1)S(1)}, u32[]{:S(2)}, u32[]{:S(2)}) collective-permute-start(bf16[2,64,512]{2,1,0:T(8,128)(2,1)S(1)} %broadcast_select_fusion.5), channel_id=1, source_target_pairs={{0,4},{4,8},{8,12},{12,16},{16,20},{20,24},{24,28},{1,5},{5,9},{9,... | collective-permute-start | bytes 393224 | tf_op jit(solution)/shard_map/while/body/eval_jaxpr/ppermute | solution.py:12
  194.2 4.4 %copy-start = (bf16[512,1000]{0,1:T(8,128)(2,1)S(1)}, bf16[512,1000]{0,1:T(8,128)(2,1)}, u32[]{:S(2)}) copy-start(bf16[512,1000]{0,1:T(8,128)(2,1)} %get-tuple-element.683) | copy-start | bytes 3072004 | tf_op jit(solution)/shard_map/while
  200.7 6.8 %collective-permute-start = (bf16[2,64,512]{2,1,0:T(8,128)(2,1)S(1)}, bf16[2,64,512]{2,1,0:T(8,128)(2,1)S(1)}, u32[]{:S(2)}, u32[]{:S(2)}) collective-permute-start(bf16[2,64,512]{2,1,0:T(8,128)(2,1)S(1)} %broadcast_select_fusion.5), channel_id=1, source_target_pairs={{0,4},{4,8},{8,12},{12,16},{16,20},{20,24},{24,28},{1,5},{5,9},{9,... | collective-permute-start | bytes 393224 | tf_op jit(solution)/shard_map/while/body/eval_jaxpr/ppermute | solution.py:12
  210.8 4.4 %copy-start = (bf16[512,1000]{0,1:T(8,128)(2,1)S(1)}, bf16[512,1000]{0,1:T(8,128)(2,1)}, u32[]{:S(2)}) copy-start(bf16[512,1000]{0,1:T(8,128)(2,1)} %get-tuple-element.683) | copy-start | bytes 3072004 | tf_op jit(solution)/shard_map/while
  217.3 8.1 %collective-permute-start = (bf16[2,64,512]{2,1,0:T(8,128)(2,1)S(1)}, bf16[2,64,512]{2,1,0:T(8,128)(2,1)S(1)}, u32[]{:S(2)}, u32[]{:S(2)}) collective-permute-start(bf16[2,64,512]{2,1,0:T(8,128)(2,1)S(1)} %broadcast_select_fusion.5), channel_id=1, source_target_pairs={{0,4},{4,8},{8,12},{12,16},{16,20},{20,24},{24,28},{1,5},{5,9},{9,... | collective-permute-start | bytes 393224 | tf_op jit(solution)/shard_map/while/body/eval_jaxpr/ppermute | solution.py:12
  228.7 4.4 %copy-start = (bf16[512,1000]{0,1:T(8,128)(2,1)S(1)}, bf16[512,1000]{0,1:T(8,128)(2,1)}, u32[]{:S(2)}) copy-start(bf16[512,1000]{0,1:T(8,128)(2,1)} %get-tuple-element.683) | copy-start | bytes 3072004 | tf_op jit(solution)/shard_map/while
  235.2 7.1 %collective-permute-start = (bf16[2,64,512]{2,1,0:T(8,128)(2,1)S(1)}, bf16[2,64,512]{2,1,0:T(8,128)(2,1)S(1)}, u32[]{:S(2)}, u32[]{:S(2)}) collective-permute-start(bf16[2,64,512]{2,1,0:T(8,128)(2,1)S(1)} %broadcast_select_fusion.5), channel_id=1, source_target_pairs={{0,4},{4,8},{8,12},{12,16},{16,20},{20,24},{24,28},{1,5},{5,9},{9,... | collective-permute-start | bytes 393224 | tf_op jit(solution)/shard_map/while/body/eval_jaxpr/ppermute | solution.py:12
  245.6 4.4 %copy-start = (bf16[512,1000]{0,1:T(8,128)(2,1)S(1)}, bf16[512,1000]{0,1:T(8,128)(2,1)}, u32[]{:S(2)}) copy-start(bf16[512,1000]{0,1:T(8,128)(2,1)} %get-tuple-element.683) | copy-start | bytes 3072004 | tf_op jit(solution)/shard_map/while
  252.1 7.1 %collective-permute-start = (bf16[2,64,512]{2,1,0:T(8,128)(2,1)S(1)}, bf16[2,64,512]{2,1,0:T(8,128)(2,1)S(1)}, u32[]{:S(2)}, u32[]{:S(2)}) collective-permute-start(bf16[2,64,512]{2,1,0:T(8,128)(2,1)S(1)} %broadcast_select_fusion.5), channel_id=1, source_target_pairs={{0,4},{4,8},{8,12},{12,16},{16,20},{20,24},{24,28},{1,5},{5,9},{9,... | collective-permute-start | bytes 393224 | tf_op jit(solution)/shard_map/while/body/eval_jaxpr/ppermute | solution.py:12
  262.4 4.4 %copy-start = (bf16[512,1000]{0,1:T(8,128)(2,1)S(1)}, bf16[512,1000]{0,1:T(8,128)(2,1)}, u32[]{:S(2)}) copy-start(bf16[512,1000]{0,1:T(8,128)(2,1)} %get-tuple-element.683) | copy-start | bytes 3072004 | tf_op jit(solution)/shard_map/while
  269.0 7.1 %collective-permute-start = (bf16[2,64,512]{2,1,0:T(8,128)(2,1)S(1)}, bf16[2,64,512]{2,1,0:T(8,128)(2,1)S(1)}, u32[]{:S(2)}, u32[]{:S(2)}) collective-permute-start(bf16[2,64,512]{2,1,0:T(8,128)(2,1)S(1)} %broadcast_select_fusion.5), channel_id=1, source_target_pairs={{0,4},{4,8},{8,12},{12,16},{16,20},{20,24},{24,28},{1,5},{5,9},{9,... | collective-permute-start | bytes 393224 | tf_op jit(solution)/shard_map/while/body/eval_jaxpr/ppermute | solution.py:12
  279.3 4.4 %copy-start = (bf16[512,1000]{0,1:T(8,128)(2,1)S(1)}, bf16[512,1000]{0,1:T(8,128)(2,1)}, u32[]{:S(2)}) copy-start(bf16[512,1000]{0,1:T(8,128)(2,1)} %get-tuple-element.683) | copy-start | bytes 3072004 | tf_op jit(solution)/shard_map/while
  285.9 6.8 %collective-permute-start = (bf16[2,64,512]{2,1,0:T(8,128)(2,1)S(1)}, bf16[2,64,512]{2,1,0:T(8,128)(2,1)S(1)}, u32[]{:S(2)}, u32[]{:S(2)}) collective-permute-start(bf16[2,64,512]{2,1,0:T(8,128)(2,1)S(1)} %broadcast_select_fusion.5), channel_id=1, source_target_pairs={{0,4},{4,8},{8,12},{12,16},{16,20},{20,24},{24,28},{1,5},{5,9},{9,... | collective-permute-start | bytes 393224 | tf_op jit(solution)/shard_map/while/body/eval_jaxpr/ppermute | solution.py:12
  296.0 4.4 %copy-start = (bf16[512,1000]{0,1:T(8,128)(2,1)S(1)}, bf16[512,1000]{0,1:T(8,128)(2,1)}, u32[]{:S(2)}) copy-start(bf16[512,1000]{0,1:T(8,128)(2,1)} %get-tuple-element.683) | copy-start | bytes 3072004 | tf_op jit(solution)/shard_map/while
  302.5 6.8 %collective-permute-start = (bf16[2,64,512]{2,1,0:T(8,128)(2,1)S(1)}, bf16[2,64,512]{2,1,0:T(8,128)(2,1)S(1)}, u32[]{:S(2)}, u32[]{:S(2)}) collective-permute-start(bf16[2,64,512]{2,1,0:T(8,128)(2,1)S(1)} %broadcast_select_fusion.5), channel_id=1, source_target_pairs={{0,4},{4,8},{8,12},{12,16},{16,20},{20,24},{24,28},{1,5},{5,9},{9,... | collective-permute-start | bytes 393224 | tf_op jit(solution)/shard_map/while/body/eval_jaxpr/ppermute | solution.py:12
  312.6 4.4 %copy-start = (bf16[512,1000]{0,1:T(8,128)(2,1)S(1)}, bf16[512,1000]{0,1:T(8,128)(2,1)}, u32[]{:S(2)}) copy-start(bf16[512,1000]{0,1:T(8,128)(2,1)} %get-tuple-element.683) | copy-start | bytes 3072004 | tf_op jit(solution)/shard_map/while
  319.1 6.8 %collective-permute-start = (bf16[2,64,512]{2,1,0:T(8,128)(2,1)S(1)}, bf16[2,64,512]{2,1,0:T(8,128)(2,1)S(1)}, u32[]{:S(2)}, u32[]{:S(2)}) collective-permute-start(bf16[2,64,512]{2,1,0:T(8,128)(2,1)S(1)} %broadcast_select_fusion.5), channel_id=1, source_target_pairs={{0,4},{4,8},{8,12},{12,16},{16,20},{20,24},{24,28},{1,5},{5,9},{9,... | collective-permute-start | bytes 393224 | tf_op jit(solution)/shard_map/while/body/eval_jaxpr/ppermute | solution.py:12
  329.3 4.4 %copy-start = (bf16[512,1000]{0,1:T(8,128)(2,1)S(1)}, bf16[512,1000]{0,1:T(8,128)(2,1)}, u32[]{:S(2)}) copy-start(bf16[512,1000]{0,1:T(8,128)(2,1)} %get-tuple-element.683) | copy-start | bytes 3072004 | tf_op jit(solution)/shard_map/while
  335.8 6.8 %collective-permute-start = (bf16[2,64,512]{2,1,0:T(8,128)(2,1)S(1)}, bf16[2,64,512]{2,1,0:T(8,128)(2,1)S(1)}, u32[]{:S(2)}, u32[]{:S(2)}) collective-permute-start(bf16[2,64,512]{2,1,0:T(8,128)(2,1)S(1)} %broadcast_select_fusion.5), channel_id=1, source_target_pairs={{0,4},{4,8},{8,12},{12,16},{16,20},{20,24},{24,28},{1,5},{5,9},{9,... | collective-permute-start | bytes 393224 | tf_op jit(solution)/shard_map/while/body/eval_jaxpr/ppermute | solution.py:12
  345.9 4.4 %copy-start = (bf16[512,1000]{0,1:T(8,128)(2,1)S(1)}, bf16[512,1000]{0,1:T(8,128)(2,1)}, u32[]{:S(2)}) copy-start(bf16[512,1000]{0,1:T(8,128)(2,1)} %get-tuple-element.683) | copy-start | bytes 3072004 | tf_op jit(solution)/shard_map/while
  352.4 6.8 %collective-permute-start = (bf16[2,64,512]{2,1,0:T(8,128)(2,1)S(1)}, bf16[2,64,512]{2,1,0:T(8,128)(2,1)S(1)}, u32[]{:S(2)}, u32[]{:S(2)}) collective-permute-start(bf16[2,64,512]{2,1,0:T(8,128)(2,1)S(1)} %broadcast_select_fusion.5), channel_id=1, source_target_pairs={{0,4},{4,8},{8,12},{12,16},{16,20},{20,24},{24,28},{1,5},{5,9},{9,... | collective-permute-start | bytes 393224 | tf_op jit(solution)/shard_map/while/body/eval_jaxpr/ppermute | solution.py:12
  362.5 4.4 %copy-start = (bf16[512,1000]{0,1:T(8,128)(2,1)S(1)}, bf16[512,1000]{0,1:T(8,128)(2,1)}, u32[]{:S(2)}) copy-start(bf16[512,1000]{0,1:T(8,128)(2,1)} %get-tuple-element.683) | copy-start | bytes 3072004 | tf_op jit(solution)/shard_map/while
  369.1 6.8 %collective-permute-start = (bf16[2,64,512]{2,1,0:T(8,128)(2,1)S(1)}, bf16[2,64,512]{2,1,0:T(8,128)(2,1)S(1)}, u32[]{:S(2)}, u32[]{:S(2)}) collective-permute-start(bf16[2,64,512]{2,1,0:T(8,128)(2,1)S(1)} %broadcast_select_fusion.5), channel_id=1, source_target_pairs={{0,4},{4,8},{8,12},{12,16},{16,20},{20,24},{24,28},{1,5},{5,9},{9,... | collective-permute-start | bytes 393224 | tf_op jit(solution)/shard_map/while/body/eval_jaxpr/ppermute | solution.py:12
  379.2 4.4 %copy-start = (bf16[512,1000]{0,1:T(8,128)(2,1)S(1)}, bf16[512,1000]{0,1:T(8,128)(2,1)}, u32[]{:S(2)}) copy-start(bf16[512,1000]{0,1:T(8,128)(2,1)} %get-tuple-element.683) | copy-start | bytes 3072004 | tf_op jit(solution)/shard_map/while
  (44 other events, 127.4 us)
where the time goes:
time: 432 us; the launch traced here: 428 us
  matrix products  125 us (29%)
  starting transfers between devices  96.1 us (22%)
  other arithmetic  83.5 us (19%)
  local copies, waits for them, and re-layouts  47.1 us (11%)
  blocking collectives  41.9 us (10%)
  loops' own time  32.7 us (8%)
    ppermute x23, starting transfers between devices, from_behind(): lax.ppermute(value, axis, [(source, source + steps) for source in range(f...  96.1 us
    dot_general x23, matrix products, mixer_block(): jnp.dot(channel_hidden, channel_two, preferred_element_type=jnp.float32)  75.1 us
    psum x1, blocking collectives, local(): return lax.psum(totals, ('aa', 'ba'))  41.9 us
    reduce_sum x46, other arithmetic, layer_norm(): center = values - jnp.mean(values, axis=-1, keepdims=True)  41.3 us
    dot_general x23, matrix products, mixer_block(): jnp.einsum('hcx,mc->hmx', token_mixing_hidden, token_second_weight, prefe...  38.9 us
    another operation x1, loops' own time, local(): final_state, totals = lax.fori_loop(0, steps_total, advance, start)  32.7 us
    slice x23, local copies, waits for them, and re-layouts, mixer_block(): second = layer_norm(mixed, gain_pair[1]).astype(jnp.bfloat16)  17.7 us
    reduce_sum x23, other arithmetic, head_loss(): return jnp.sum(total - picked)  15.7 us
  transfers between devices with their start and end apart: 23, of which 3 were waited for; matrix products, arithmetic and copies ran while one was open for 11% of the time, Pallas kernels for 0%

commit v1 on v0

v1 whole, which is shorter than its diff:
```python
import functools

import jax
import jax.numpy as jnp
from jax import lax
from jax.experimental import pallas as pl
from jax.experimental.pallas import tpu as pltpu
from jax.sharding import PartitionSpec as P

UNIT = 4
QUARTERS = 4
MESH = pl.DeviceIdType.MESH
GELU_A = 0.7978845608028654
GELU_B = 0.044715 * GELU_A


def layer_norm(values, gain):
    center = values - jnp.mean(values, axis=-1, keepdims=True)
    spread = jnp.mean(center * center, axis=-1, keepdims=True)
    return center * lax.rsqrt(spread + 1e-06) * gain


def gelu(x, half):
    bent = jnp.tanh(x * (GELU_A + GELU_B * (x * x)))
    scaled = x * half
    return scaled + scaled * bent


def dot(a, b):
    return jnp.dot(a, b, preferred_element_type=jnp.float32)


def kernel(
    sections,
    shards,
    depths,
    widths,
    labels,
    patches,
    token_first,
    token_second,
    channel_first,
    channel_second,
    gains,
    final_gain,
    head_weight,
    out,
    inbox,
    outbox,
    token_first_t,
    pooled,
    share,
    landing,
    send_sem,
    recv_sem,
    share_sem,
    landing_sem,
):
    section = lax.axis_index("aa")
    shard = lax.axis_index("ba")
    last = sections - 1
    images, _, width_model = patches.shape
    candidates = depths.shape[0]
    units = candidates * images
    hidden_units = channel_first.shape[2]
    quarter = hidden_units // QUARTERS

    barrier = pltpu.get_barrier_semaphore()

    def greet(aa, ba):
        pl.semaphore_signal(barrier, inc=1, device_id=(aa, ba), device_id_type=MESH)

    @pl.when(section > 0)
    def _():
        greet(section - 1, shard)

    for other in range(shards):

        @pl.when(jnp.logical_or(section < last, shard != other))
        def _():
            greet(last, other)

    @pl.when(section < last)
    def _():
        pl.semaphore_wait(barrier, 1)

    @pl.when(section == last)
    def _():
        pl.semaphore_wait(barrier, sections * shards - 1)

    token_first_t[...] = token_first[0].T

    def hop(unit):
        return pltpu.make_async_remote_copy(
            src_ref=outbox.at[unit],
            dst_ref=inbox.at[unit],
            send_sem=send_sem.at[unit],
            recv_sem=recv_sem.at[unit],
            device_id=(lax.rem(section + 1, sections), shard),
            device_id_type=MESH,
        )

    def step(unit, carry):
        candidate = unit // images
        image = unit % images

        @pl.when(section == 0)
        def _():
            inbox[unit] = patches[image]

        @pl.when(section > 0)
        def _():
            hop(unit).wait_recv()

        width = widths[candidate, section]
        active = section % UNIT < depths[candidate, section // UNIT]
        state = inbox[unit]
        floats = state.astype(jnp.float32)
        normed = layer_norm(floats, gains[0, 0:1, :]).astype(jnp.bfloat16)
        token_hidden = gelu(dot(token_first_t[...], normed), 0.5).astype(jnp.bfloat16)
        mixed = floats + dot(token_second[0], token_hidden)
        second = layer_norm(mixed, gains[0, 1:2, :]).astype(jnp.bfloat16)
        total = mixed
        for index in range(QUARTERS):
            span = slice(index * quarter, (index + 1) * quarter)
            half = jnp.where(index < width, 0.5, 0.0)
            hidden = gelu(dot(second, channel_first[0, :, span]), half)
            total = total + dot(hidden.astype(jnp.bfloat16), channel_second[0, span, :])
        updated = jnp.where(active, total.astype(jnp.bfloat16), state)
        outbox[unit] = updated

        @pl.when(section < last)
        def _():
            hop(unit).start()

        @pl.when(section == last)
        def _():
            final = layer_norm(outbox[unit].astype(jnp.float32), final_gain[...])
            row = image * candidates + candidate
            pooled[pl.ds(row, 1), :] = jnp.mean(final, axis=0, keepdims=True)

        return carry

    lax.fori_loop(0, units, step, 0)

    def tell(aa, ba):
        return pltpu.make_async_remote_copy(
            src_ref=share,
            dst_ref=landing.at[shard],
            send_sem=share_sem.at[aa * shards + ba],
            recv_sem=landing_sem.at[shard],
            device_id=(aa, ba),
            device_id_type=MESH,
        )

    def each_other(act):
        def visit(target, carry):
            aa, ba = target // shards, target % shards

            @pl.when(jnp.logical_or(aa != section, ba != shard))
            def _():
                act(tell(aa, ba))

            return carry

        lax.fori_loop(0, sections * shards, visit, 0)

    @pl.when(section == last)
    def _():
        logits = dot(pooled[...].astype(jnp.bfloat16), head_weight[...])
        top = jnp.max(logits, axis=-1, keepdims=True)
        total = top + jnp.log(jnp.sum(jnp.exp(logits - top), axis=-1, keepdims=True))
        rows = lax.broadcasted_iota(jnp.int32, logits.shape, 0)
        classes = lax.broadcasted_iota(jnp.int32, logits.shape, 1)
        wanted = jnp.full(logits.shape, labels[0], jnp.int32)
        for image in range(1, images):
            wanted = jnp.where(rows >= image * candidates, labels[image], wanted)
        picked = jnp.sum(
            jnp.where(classes == wanted, logits, 0.0), axis=-1, keepdims=True
        )
        losses = total - picked
        summed = losses[:candidates]
        for image in range(1, images):
            summed = summed + losses[image * candidates : (image + 1) * candidates]
        lanes = out.shape[1]
        rows = lax.broadcasted_iota(jnp.int32, (candidates, lanes), 0)
        cols = lax.broadcasted_iota(jnp.int32, (candidates, lanes), 1)
        spread = jnp.broadcast_to(summed, (candidates, lanes))
        line = jnp.sum(jnp.where(rows == cols, spread, 0.0), axis=0, keepdims=True)
        share[...] = line
        landing[shard] = line
        each_other(lambda copy: copy.start())
        each_other(lambda copy: copy.wait_send())

    @pl.when(section < last)
    def _():
        def drain(unit, carry):
            hop(unit).wait_send()
            return carry

        lax.fori_loop(0, units, drain, 0)

    for origin in range(shards):

        @pl.when(jnp.logical_or(section < last, shard != origin))
        def _():
            pltpu.make_async_remote_copy(
                src_ref=share,
                dst_ref=landing.at[origin],
                send_sem=share_sem.at[0],
                recv_sem=landing_sem.at[origin],
                device_id=(last, origin),
                device_id_type=MESH,
            ).wait_recv()

    result = landing[0]
    for origin in range(1, shards):
        result = result + landing[origin]
    out[...] = result


def solution(mesh):
    sections, shards = mesh.shape["aa"], mesh.shape["ba"]

    def local(
        patches,
        token_first,
        token_second,
        channel_first,
        channel_second,
        gains,
        final_gain,
        head_weight,
        depths,
        widths,
        labels,
    ):
        images, patch_count, model = patches.shape
        candidates = depths.shape[0]
        units = candidates * images
        lanes = pl.cdiv(candidates, 128) * 128
        smem = pl.BlockSpec(memory_space=pltpu.SMEM)
        vmem = pl.BlockSpec(memory_space=pltpu.VMEM)
        line = pl.pallas_call(
            functools.partial(kernel, sections, shards),
            out_shape=jax.ShapeDtypeStruct((1, lanes), jnp.float32),
            in_specs=[smem] * 3 + [vmem] * 8,
            out_specs=vmem,
            scratch_shapes=[
                pltpu.VMEM((units, patch_count, model), jnp.bfloat16),
                pltpu.VMEM((units, patch_count, model), jnp.bfloat16),
                pltpu.VMEM((token_first.shape[2], patch_count), jnp.bfloat16),
                pltpu.VMEM((units, model), jnp.float32),
                pltpu.VMEM((1, lanes), jnp.float32),
                pltpu.VMEM((shards, 1, lanes), jnp.float32),
                pltpu.SemaphoreType.DMA((units,)),
                pltpu.SemaphoreType.DMA((units,)),
                pltpu.SemaphoreType.DMA((sections * shards,)),
                pltpu.SemaphoreType.DMA((shards,)),
            ],
            compiler_params=pltpu.CompilerParams(
                collective_id=0, has_side_effects=True
            ),
        )(
            depths,
            widths,
            labels,
            patches,
            token_first,
            token_second,
            channel_first,
            channel_second,
            gains,
            final_gain[None, :],
            head_weight,
        )
        return line[0, :candidates]

    return jax.shard_map(
        local,
        mesh=mesh,
        in_specs=(
            P("ba", None, None),
            P("aa", None, None),
            P("aa", None, None),
            P("aa", None, None),
            P("aa", None, None),
            P("aa", None, None),
            P(),
            P(),
            P(),
            P(),
            P("ba"),
        ),
        out_specs=P(),
        check_vma=False,
    )
```

time: 432 us -> 128 us (0.30); the launches traced: 428 us -> 128 us
  matrix products: 125 us -> 0 us
  Pallas kernels: 0 us -> 122 us
  starting transfers between devices: 96.1 us -> 0 us
  other arithmetic: 83.5 us -> 0 us
  blocking collectives: 41.9 us -> 0 us
  local copies, waits for them, and re-layouts: 47.1 us -> 6.11 us
  loops' own time: 32.7 us -> 0 us
    dot_general x69 -> x0, matrix products: 125 us -> none  [the longest x23 75.1 us: mixer_block(): jnp.dot(channel_hidden, channel_two, preferred_element_type=jnp.float32)]
    pallas_call x0 -> x1, Pallas kernels: none -> 122 us  [local(): pl.pallas_call(functools.partial(kernel, sections, shards), out_shape=jax...]
    ppermute x23 -> x0, starting transfers between devices: 96.1 us -> none  [from_behind(): lax.ppermute(value, axis, [(source, source + steps) for source in range(f...]
    reduce_sum x186 -> x0, other arithmetic: 79 us -> none  [the longest x46 41.3 us: layer_norm(): center = values - jnp.mean(values, axis=-1, keepdims=True)]
    psum x1 -> x0, blocking collectives: 41.9 us -> none  [local(): return lax.psum(totals, ('aa', 'ba'))]
    another operation x1 -> x0, loops' own time: 32.7 us -> none  [local(): final_state, totals = lax.fori_loop(0, steps_total, advance, start)]
    dynamic_slice x46 -> x0, local copies, waits for them, and re-layouts: 29 us -> none  [the longest x23 14.9 us: advance(): active = active_here[candidate]]
    slice x23 -> x0, local copies, waits for them, and re-layouts: 17.7 us -> none  [mixer_block(): second = layer_norm(mixed, gain_pair[1]).astype(jnp.bfloat16)]
  transfers between devices with their start and end apart: 23 -> 0, of which waited for: 3 -> 0; matrix products, arithmetic and copies ran while one was open for 11% -> 0% of each run, Pallas kernels for 0% -> 0%
where the time goes in v1:
time: 128 us
  Pallas kernels  122 us (95%)
  local copies, waits for them, and re-layouts  6.11 us (5%)
    pallas_call x1, Pallas kernels, local(): pl.pallas_call(functools.partial(kernel, sections, shards), out_shape=jax...  122 us
    unnamed x3, local copies, waits for them, and re-layouts  4.97 us

profile of v1, /device:TPU:0, one launch (start us, length us, event | category | flops | bytes accessed | tf_op | source)
XLA Modules:
  0.0 128.1 jit_solution(2494661913760842383)
XLA Ops:
  0.0 1.3 %copy.12.depths = s32[16,2]{1,0:T(8,128)} copy(s32[16,2]{0,1:T(2,128)} %param.19) | data formatting | bytes 256 | tf_op args[8]
  1.3 1.4 %copy.13.widths = s32[16,8]{1,0:T(8,128)} copy(s32[16,8]{0,1:T(8,128)} %param.20) | data formatting | bytes 1024 | tf_op args[9]
  2.7 2.3 %copy.14.head_weight = bf16[512,1000]{1,0:T(8,128)(2,1)} copy(bf16[512,1000]{0,1:T(8,128)(2,1)} %param.18) | data formatting | bytes 2048000 | tf_op args[7]
  5.0 122.0 %shard_map.109 = f32[1,128]{1,0:T(1,128)} custom-call(s32[16,2]{1,0:T(8,128)} %copy.12.depths, s32[16,8]{1,0:T(8,128)} %copy.13.widths, s32[2]{0:T(128)} %labels.1, bf16[2,64,512]{2,1,0:T(8,128)(2,1)} %patches.1, bf16[1,64,256]{2,1,0:T(8,128)(2,1)} %token_first.1, bf16[1,64,256]{2,1,0:T(8,128)(2,1)} %token_second.1, bf16[1,512,2048]{2,1,0:T(8,128)(2,1)} %channel_first.1, ...), custom_call_target="tpu_custom_call" | custom-call | tf_op jit(solution)/shard_map/pallas_call | solution.py:244
  127.0 1.1 slice_bitcast_fusion

commit v2 on v1

--- a/solution.py
+++ b/solution.py
@@ -43,11 +43,16 @@
     channel_second,
     gains,
     final_gain,
-    head_weight,
+    head_weight_t,
     out,
     inbox,
     outbox,
-    token_first_t,
+    token_one,
+    token_two,
+    channel_one,
+    channel_two,
+    head,
+    token_one_t,
     pooled,
     share,
     landing,
@@ -55,16 +60,36 @@
     recv_sem,
     share_sem,
     landing_sem,
+    load_sem,
 ):
     section = lax.axis_index("aa")
     shard = lax.axis_index("ba")
     last = sections - 1
-    images, _, width_model = patches.shape
-    candidates = depths.shape[0]
+    images, patch_count, model = patches.shape
+    candidates = depths.shape[1]
     units = candidates * images
     hidden_units = channel_first.shape[2]
     quarter = hidden_units // QUARTERS
 
+    loads = [
+        pltpu.make_async_copy(source.at[0], target, load_sem.at[index])
+        for index, (source, target) in enumerate(
+            (
+                (token_first, token_one),
+                (token_second, token_two),
+                (channel_first, channel_one),
+                (channel_second, channel_two),
+            )
+        )
+    ]
+    head_load = pltpu.make_async_copy(head_weight_t, head, load_sem.at[4])
+    for load in loads:
+        load.start()
+
+    @pl.when(section == last)
+    def _():
+        head_load.start()
+
     barrier = pltpu.get_barrier_semaphore()
 
     def greet(aa, ba):
@@ -88,7 +113,9 @@
     def _():
         pl.semaphore_wait(barrier, sections * shards - 1)
 
-    token_first_t[...] = token_first[0].T
+    loads[0].wait()
+    token_one_t[...] = token_one[...].T
+    loads[1].wait()
 
     def hop(unit):
         return pltpu.make_async_remote_copy(
@@ -100,48 +127,69 @@
             device_id_type=MESH,
         )
 
-    def step(unit, carry):
-        candidate = unit // images
-        image = unit % images
+    lane_of_hidden = lax.broadcasted_iota(jnp.int32, (1, hidden_units), 1)
+
+    def step(candidate, carry):
+        first = candidate * images
 
         @pl.when(section == 0)
         def _():
-            inbox[unit] = patches[image]
+            for image in range(images):
+                inbox[first + image] = patches[image]
 
         @pl.when(section > 0)
         def _():
-            hop(unit).wait_recv()
-
-        width = widths[candidate, section]
-        active = section % UNIT < depths[candidate, section // UNIT]
-        state = inbox[unit]
-        floats = state.astype(jnp.float32)
-        normed = layer_norm(floats, gains[0, 0:1, :]).astype(jnp.bfloat16)
-        token_hidden = gelu(dot(token_first_t[...], normed), 0.5).astype(jnp.bfloat16)
-        mixed = floats + dot(token_second[0], token_hidden)
+            for image in range(images):
+                hop(first + image).wait_recv()
+
+        active = section % UNIT < depths[section // UNIT, candidate]
+        half = jnp.where(lane_of_hidden < widths[section, candidate] * quarter, 0.5, 0.0)
+        states = [inbox[first + image] for image in range(images)]
+        floats = [state.astype(jnp.float32) for state in states]
+        normed = jnp.concatenate(
+            [layer_norm(value, gains[0, 0:1, :]).astype(jnp.bfloat16) for value in floats],
+            axis=1,
+        )
+        token_hidden = gelu(dot(token_one_t[...], normed), 0.5).astype(jnp.bfloat16)
+        token_part = dot(token_two[...], token_hidden)
+        mixed = jnp.concatenate(
+            [
+                floats[image] + token_part[:, image * model : (image + 1) * model]
+                for image in range(images)
+            ],
+            axis=0,
+        )
         second = layer_norm(mixed, gains[0, 1:2, :]).astype(jnp.bfloat16)
-        total = mixed
-        for index in range(QUARTERS):
-            span = slice(index * quarter, (index + 1) * quarter)
-            half = jnp.where(index < width, 0.5, 0.0)
-            hidden = gelu(dot(second, channel_first[0, :, span]), half)
-            total = total + dot(hidden.astype(jnp.bfloat16), channel_second[0, span, :])
-        updated = jnp.where(active, total.astype(jnp.bfloat16), state)
-        outbox[unit] = updated
+
+        @pl.when(candidate == 0)
+        def _():
+            loads[2].wait()
+            loads[3].wait()
+
+        hidden = gelu(dot(second, channel_one[...]), half).astype(jnp.bfloat16)
+        total = (mixed + dot(hidden, channel_two[...])).astype(jnp.bfloat16)
+        for image in range(images):
+            rows = slice(image * patch_count, (image + 1) * patch_count)
+            outbox[first + image] = jnp.where(active, total[rows], states[image])
 
         @pl.when(section < last)
         def _():
-            hop(unit).start()
+            for image in range(images):
+                hop(first + image).start()
 
         @pl.when(section == last)
         def _():
-            final = layer_norm(outbox[unit].astype(jnp.float32), final_gain[...])
-            row = image * candidates + candidate
-            pooled[pl.ds(row, 1), :] = jnp.mean(final, axis=0, keepdims=True)
+            for image in range(images):
+                final = layer_norm(
+                    outbox[first + image].astype(jnp.float32), final_gain[...]
+                )
+                pooled[pl.ds(image * candidates + candidate, 1), :] = jnp.mean(
+                    final, axis=0, keepdims=True
+                )
 
         return carry
 
-    lax.fori_loop(0, units, step, 0)
+    lax.fori_loop(0, candidates, step, 0)
 
     def tell(aa, ba):
         return pltpu.make_async_remote_copy(
@@ -167,7 +215,13 @@
 
     @pl.when(section == last)
     def _():
-        logits = dot(pooled[...].astype(jnp.bfloat16), head_weight[...])
+        head_load.wait()
+        logits = lax.dot_general(
+            pooled[...].astype(jnp.bfloat16),
+            head[...],
+            (((1,), (1,)), ((), ())),
+            preferred_element_type=jnp.float32,
+        )
         top = jnp.max(logits, axis=-1, keepdims=True)
         total = top + jnp.log(jnp.sum(jnp.exp(logits - top), axis=-1, keepdims=True))
         rows = lax.broadcasted_iota(jnp.int32, logits.shape, 0)
@@ -241,14 +295,20 @@
         lanes = pl.cdiv(candidates, 128) * 128
         smem = pl.BlockSpec(memory_space=pltpu.SMEM)
         vmem = pl.BlockSpec(memory_space=pltpu.VMEM)
+        hbm = pl.BlockSpec(memory_space=pl.ANY)
         line = pl.pallas_call(
             functools.partial(kernel, sections, shards),
             out_shape=jax.ShapeDtypeStruct((1, lanes), jnp.float32),
-            in_specs=[smem] * 3 + [vmem] * 8,
+            in_specs=[smem] * 3 + [vmem] + [hbm] * 4 + [vmem] * 2 + [hbm],
             out_specs=vmem,
             scratch_shapes=[
                 pltpu.VMEM((units, patch_count, model), jnp.bfloat16),
                 pltpu.VMEM((units, patch_count, model), jnp.bfloat16),
+                pltpu.VMEM(token_first.shape[1:], jnp.bfloat16),
+                pltpu.VMEM(token_second.shape[1:], jnp.bfloat16),
+                pltpu.VMEM(channel_first.shape[1:], jnp.bfloat16),
+                pltpu.VMEM(channel_second.shape[1:], jnp.bfloat16),
+                pltpu.VMEM(head_weight.shape[::-1], jnp.bfloat16),
                 pltpu.VMEM((token_first.shape[2], patch_count), jnp.bfloat16),
                 pltpu.VMEM((units, model), jnp.float32),
                 pltpu.VMEM((1, lanes), jnp.float32),
@@ -257,13 +317,14 @@
                 pltpu.SemaphoreType.DMA((units,)),
                 pltpu.SemaphoreType.DMA((sections * shards,)),
                 pltpu.SemaphoreType.DMA((shards,)),
+                pltpu.SemaphoreType.DMA((5,)),
             ],
             compiler_params=pltpu.CompilerParams(
                 collective_id=0, has_side_effects=True
             ),
         )(
-            depths,
-            widths,
+            depths.T,
+            widths.T,
             labels,
             patches,
             token_first,
@@ -272,7 +333,7 @@
             channel_second,
             gains,
             final_gain[None, :],
-            head_weight,
+            head_weight.T,
         )
         return line[0, :candidates]
 

time: 128 us -> 103 us (0.80)
  Pallas kernels: 122 us -> 102 us
  local copies, waits for them, and re-layouts: 6.11 us -> 1.19 us
    pallas_call x1, Pallas kernels: 122 us -> 102 us  [local(): pl.pallas_call(functools.partial(kernel, sections, shards), out_shape=jax...]
    unnamed x3 -> x0, local copies, waits for them, and re-layouts: 4.97 us -> none
where the time goes in v2:
time: 103 us
  Pallas kernels  102 us (99%)
  local copies, waits for them, and re-layouts  1.19 us (1%)
    pallas_call x1, Pallas kernels, local(): pl.pallas_call(functools.partial(kernel, sections, shards), out_shape=jax...  102 us

profile of v2, /device:TPU:0, one launch (start us, length us, event | category | flops | bytes accessed | tf_op | source)
XLA Modules:
  0.0 103.1 jit_solution(9297327995151875287)
XLA Ops:
  0.0 101.9 %shard_map.109 = f32[1,128]{1,0:T(1,128)} custom-call(s32[2,16]{1,0:T(2,128)} %bitcast.9, s32[8,16]{1,0:T(8,128)} %bitcast.7, s32[2]{0:T(128)} %labels.1, bf16[2,64,512]{2,1,0:T(8,128)(2,1)} %patches.1, bf16[1,64,256]{2,1,0:T(8,128)(2,1)} %token_first.1, bf16[1,64,256]{2,1,0:T(8,128)(2,1)} %token_second.1, bf16[1,512,2048]{2,1,0:T(8,128)(2,1)} %channel_first.1, ...), custom_call_target="tpu_custom_call" | custom-call | tf_op jit(solution)/shard_map/pallas_call | solution.py:299
  101.9 1.2 %slice_bitcast_fusion = f32[16]{0:T(128)} fusion(f32[1,128]{1,0:T(1,128)} %shard_map.109), kind=kLoop, calls=%fused_computation | loop fusion | bytes 128 | tf_op jit(solution)/shard_map/squeeze | solution.py:338

commit v3 on v2

--- a/solution.py
+++ b/solution.py
@@ -129,22 +129,28 @@
 
     lane_of_hidden = lax.broadcasted_iota(jnp.int32, (1, hidden_units), 1)
 
-    def step(candidate, carry):
-        first = candidate * images
-
-        @pl.when(section == 0)
-        def _():
-            for image in range(images):
-                inbox[first + image] = patches[image]
-
-        @pl.when(section > 0)
-        def _():
-            for image in range(images):
+    def step(group, finish, index, carry):
+        first = index * group
+        candidate = first // images
+
+        if finish:
+            for image in range(group):
                 hop(first + image).wait_recv()
+        else:
+
+            @pl.when(section == 0)
+            def _():
+                for image in range(group):
+                    inbox[first + image] = patches[(first + image) % images]
+
+            @pl.when(section > 0)
+            def _():
+                for image in range(group):
+                    hop(first + image).wait_recv()
 
         active = section % UNIT < depths[section // UNIT, candidate]
         half = jnp.where(lane_of_hidden < widths[section, candidate] * quarter, 0.5, 0.0)
-        states = [inbox[first + image] for image in range(images)]
+        states = [inbox[first + image] for image in range(group)]
         floats = [state.astype(jnp.float32) for state in states]
         normed = jnp.concatenate(
             [layer_norm(value, gains[0, 0:1, :]).astype(jnp.bfloat16) for value in floats],
@@ -155,41 +161,35 @@
         mixed = jnp.concatenate(
             [
                 floats[image] + token_part[:, image * model : (image + 1) * model]
-                for image in range(images)
+                for image in range(group)
             ],
             axis=0,
         )
         second = layer_norm(mixed, gains[0, 1:2, :]).astype(jnp.bfloat16)
 
-        @pl.when(candidate == 0)
-        def _():
-            loads[2].wait()
-            loads[3].wait()
-
         hidden = gelu(dot(second, channel_one[...]), half).astype(jnp.bfloat16)
         total = (mixed + dot(hidden, channel_two[...])).astype(jnp.bfloat16)
-        for image in range(images):
+        for image in range(group):
             rows = slice(image * patch_count, (image + 1) * patch_count)
-            outbox[first + image] = jnp.where(active, total[rows], states[image])
-
-        @pl.when(section < last)
-        def _():
-            for image in range(images):
+            updated = jnp.where(active, total[rows], states[image])
+            if finish:
+                final = layer_norm(updated.astype(jnp.float32), final_gain[...])
+                row = (first + image) % images * candidates + candidate
+                pooled[pl.ds(row, 1), :] = jnp.mean(final, axis=0, keepdims=True)
+            else:
+                outbox[first + image] = updated
                 hop(first + image).start()
-
-        @pl.when(section == last)
-        def _():
-            for image in range(images):
-                final = layer_norm(
-                    outbox[first + image].astype(jnp.float32), final_gain[...]
-                )
-                pooled[pl.ds(image * candidates + candidate, 1), :] = jnp.mean(
-                    final, axis=0, keepdims=True
-                )
-
         return carry
 
-    lax.fori_loop(0, candidates, step, 0)
+    loads[2].wait()
+    loads[3].wait()
+    @pl.when(section < last)
+    def _():
+        lax.fori_loop(0, units, functools.partial(step, 1, False), 0)
+
+    @pl.when(section == last)
+    def _():
+        lax.fori_loop(0, candidates, functools.partial(step, images, True), 0)
 
     def tell(aa, ba):
         return pltpu.make_async_remote_copy(

time: 103 us -> 102 us (level)
  Pallas kernels: 102 us -> 100 us
    pallas_call x1, Pallas kernels: 102 us -> 100 us  [local(): pl.pallas_call(functools.partial(kernel, sections, shards), out_shape=jax...]
where the time goes in v3:
time: 102 us; the launch traced here: 101 us
  Pallas kernels  100 us (98%)
  local copies, waits for them, and re-layouts  1.19 us (1%)
    pallas_call x1, Pallas kernels, local(): pl.pallas_call(functools.partial(kernel, sections, shards), out_shape=jax...  100 us

profile of v3, /device:TPU:0, one launch (start us, length us, event | category | flops | bytes accessed | tf_op | source)
XLA Modules:
  0.0 101.4 jit_solution(6930161463115857701)
XLA Ops:
  0.0 100.2 %shard_map.109 = f32[1,128]{1,0:T(1,128)} custom-call(s32[2,16]{1,0:T(2,128)} %bitcast.9, s32[8,16]{1,0:T(8,128)} %bitcast.7, s32[2]{0:T(128)} %labels.1, bf16[2,64,512]{2,1,0:T(8,128)(2,1)} %patches.1, bf16[1,64,256]{2,1,0:T(8,128)(2,1)} %token_first.1, bf16[1,64,256]{2,1,0:T(8,128)(2,1)} %token_second.1, bf16[1,512,2048]{2,1,0:T(8,128)(2,1)} %channel_first.1, ...), custom_call_target="tpu_custom_call" | custom-call | tf_op jit(solution)/shard_map/pallas_call | solution.py:299
  100.2 1.2 %slice_bitcast_fusion = f32[16]{0:T(128)} fusion(f32[1,128]{1,0:T(1,128)} %shard_map.109), kind=kLoop, calls=%fused_computation | loop fusion | bytes 128 | tf_op jit(solution)/shard_map/squeeze | solution.py:338
